TPU v7x, 256 devices: a whole 4x4x8 slice. The times are simulated.
256 devices in a mesh: out: 32 (over x, z_hi, core), in: 8 (over z_lo, y).
Axes of the slice: x: 4, y: 4, z: 8 (z_hi: 4, z_lo: 2; z = z_hi * 2 + z_lo), core: 2. Of those that a mesh axis runs over, the one named last changes fastest.
Arguments:
- slopes: bfloat16 [256, 163840], P('out', 'in'), may hold values from -6 to 6
- cols_first: int32 [128, 64], P(None, 'in'), may hold values from 0 to 79
- count_first: int32 [128, 8], P('out', 'in'), may hold values from 1 to 8
- weight_first: bfloat16 [128, 64, 256, 256], P('out', 'in'), may hold values from -0.0625 to 0.0625
- bias_first: float32 [32768], P(('out', 'in')), may hold values from -3 to 3
- cols_second: int32 [128, 32], P('out', 'in'), may hold values from 0 to 15
- count_second: int32 [128, 8], P('out', 'in'), may hold values from 1 to 4
- weight_second: bfloat16 [128, 32, 256, 256], P('out', 'in'), may hold values from -0.09375 to 0.09375
- bias_second: float32 [32768], P(('out', 'in')), may hold values from -3 to 3
- cotangent: bfloat16 [256, 32768], P(None, ('out', 'in')), may hold values from -6 to 6
Outputs:
- estimate: bfloat16 [256, 32768], P(None, ('out', 'in'))
- grad_first: bfloat16 [128, 64, 256, 256], P('out', 'in')
- grad_second: bfloat16 [128, 32, 256, 256], P('out', 'in')
Inputs may be any that keep to these rules, and one draw needn't show every extreme that they name: `cols_first`: A local block index within the range of slopes of the slot's in index. `count_first`: slots of a block row at or after this count, within one in range, are not used. `cols_second`: A local block index within the range of reordered hidden units of the slot's in index. `count_second`: slots of a block row at or after this count, within one in range, are not used.
All inputs are finite; a program needn't handle non-finite values.
Results may differ from a plain program's by a relative error of at most 0.025.
Values may be sent and summed in bfloat16 or wider, within the bound.
No kernel may reach another device: no remote copies, remote signals or barrier semaphores. Data moves between devices by JAX's collectives and lax.ppermute only.
A program may use at most 128 MiB of HBM per device.

v0:
```python
import jax
import jax.numpy as jnp
from jax import lax
from jax.sharding import PartitionSpec as P

BLK = 256
KD1 = 8
KD2 = 4


def shards(
    slopes,
    cols_first,
    count_first,
    weight_first,
    bias_first,
    cols_second,
    count_second,
    weight_second,
    bias_second,
    cotangent,
):
    rows = weight_first.shape[0]
    live_first = jnp.arange(KD1, dtype=jnp.int32)[None, :] < count_first
    live_second = jnp.arange(KD2, dtype=jnp.int32)[None, :] < count_second
    masked_first = weight_first * live_first.astype(jnp.bfloat16)[:, :, None, None]
    masked_second = weight_second * live_second.astype(jnp.bfloat16)[:, :, None, None]
    gathered = lax.all_gather(slopes, "out", axis=0, tiled=True)
    frames = gathered.shape[0]
    slope_blocks = gathered.reshape(frames, -1, BLK)
    own_cols = lax.dynamic_slice_in_dim(cols_first, lax.axis_index("out") * rows, rows, 0)
    panels_first = jnp.take(slope_blocks, own_cols.reshape(-1), axis=1).reshape(
        frames, rows, KD1, BLK
    )
    partial_first = jnp.einsum(
        "frkb,rkbo->fro", panels_first, masked_first, preferred_element_type=jnp.float32
    ).reshape(frames, rows * BLK)
    summed_first = lax.psum_scatter(partial_first, "in", scatter_dimension=1, tiled=True)
    hidden_first = jnp.tanh(summed_first + bias_first[None, :]).astype(jnp.bfloat16)
    second_input = lax.all_gather(hidden_first, "out", axis=1, tiled=True)
    hidden_blocks = second_input.reshape(frames, -1, BLK)
    panels_second = jnp.take(hidden_blocks, cols_second.reshape(-1), axis=1).reshape(
        frames, rows, KD2, BLK
    )
    partial_second = jnp.einsum(
        "frkb,rkbo->fro", panels_second, masked_second, preferred_element_type=jnp.float32
    ).reshape(frames, rows * BLK)
    summed_second = lax.psum_scatter(partial_second, "in", scatter_dimension=1, tiled=True)
    estimate = jnp.tanh(summed_second + bias_second[None, :]).astype(jnp.bfloat16)
    est32 = estimate.astype(jnp.float32)
    delta_second = (cotangent.astype(jnp.float32) * (1.0 - est32 * est32)).astype(jnp.bfloat16)
    rows_second = lax.all_gather(delta_second, "in", axis=1, tiled=True).reshape(frames, rows, BLK)
    grad_second = jnp.einsum(
        "frkb,fro->rkbo", panels_second, rows_second, preferred_element_type=jnp.float32
    )
    grad_second = (grad_second * live_second.astype(jnp.float32)[:, :, None, None]).astype(
        jnp.bfloat16
    )
    adjoint = jnp.einsum(
        "fro,rkbo->frkb", rows_second, masked_second, preferred_element_type=jnp.float32
    ).reshape(frames, rows * KD2, BLK)
    selector = (
        cols_second.reshape(-1)[:, None]
        == jnp.arange(hidden_blocks.shape[1], dtype=jnp.int32)[None, :]
    ).astype(jnp.float32)
    spread = jnp.einsum("fjb,jc->fcb", adjoint, selector, precision=lax.Precision.HIGHEST).reshape(
        frames, -1
    )
    back_first = lax.psum_scatter(
        spread.astype(jnp.bfloat16), "out", scatter_dimension=1, tiled=True
    ).astype(jnp.float32)
    hid32 = hidden_first.astype(jnp.float32)
    delta_first = (back_first * (1.0 - hid32 * hid32)).astype(jnp.bfloat16)
    rows_first = lax.all_gather(delta_first, "in", axis=1, tiled=True).reshape(frames, rows, BLK)
    grad_first = jnp.einsum(
        "frkb,fro->rkbo", panels_first, rows_first, preferred_element_type=jnp.float32
    )
    grad_first = (grad_first * live_first.astype(jnp.float32)[:, :, None, None]).astype(
        jnp.bfloat16
    )
    return (estimate, grad_first, grad_second)


def solution(mesh):
    return jax.shard_map(
        shards,
        mesh=mesh,
        in_specs=(
            P("out", "in"),
            P(None, "in"),
            P("out", "in"),
            P("out", "in", None, None),
            P(("out", "in")),
            P("out", "in"),
            P("out", "in"),
            P("out", "in", None, None),
            P(("out", "in")),
            P(None, ("out", "in")),
        ),
        out_specs=(P(None, ("out", "in")), P("out", "in", None, None), P("out", "in", None, None)),
        check_vma=False,
    )
```

profile of v0, /device:TPU:24, one launch (start us, length us, event | category | flops | bytes accessed | tf_op | source)
XLA Modules:
  0.0 476.3 jit_solution(1294169107600888628)
XLA Ops:
  7.2 0.0 all-gather.3.cloned.1.call-start
  7.2 0.7 all-gather.3.cloned.1.call-update
  7.9 0.0 reduce-scatter.4.cloned.1.call-start
  7.9 0.8 compare_and_fusion
  8.7 0.1 copy.57
  8.8 0.1 copy.59
  8.9 0.1 reshape.203
  9.0 0.7 fusion.17
  9.7 93.1 %all-gather.3.cloned.1.call-done = bf16[256,20480]{1,0:T(8,128)(2,1)} async-done(((bf16[8,20480]{1,0:T(8,128)(2,1)}), bf16[256,20480]{1,0:T(8,128)(2,1)}) %all-gather.3.cloned.1.call-update) | async-done | bytes 10485776 | tf_op jit(solution)/shard_map/all_gather | solution.py:28
  102.8 13.8 %copy.58 = bf16[256,20480]{0,1:T(8,128)(2,1)} copy(bf16[256,20480]{1,0:T(8,128)(2,1)} %all-gather.3.cloned.1.call-done) | data formatting | bytes 20971520 | tf_op jit(solution)/shard_map/all_gather | solution.py:28
  116.5 14.4 %copy.60 = bf16[256,80,256]{2,0,1:T(8,128)(2,1)} copy(bf16[256,80,256]{0,2,1:T(8,128)(2,1)} %bitcast.50) | data formatting | bytes 20971520 | tf_op jit(solution)/shard_map/reshape | solution.py:30
  130.9 6.8 %gather_fusion = bf16[32,256,256]{2,1,0:T(8,128)(2,1)} fusion(bf16[256,80,256]{2,0,1:T(8,128)(2,1)} %copy.60, s32[1024]{0:T(1024)S(1)} %pad_clamp_fusion.1), kind=kCustom, calls=%fused_computation | custom fusion | bytes 8388736 | tf_op jit(solution)/shard_map/jit(_take)/gather | solution.py:32
  137.7 6.2 %copy.61 = bf16[256,4,8,256]{0,3,2,1:T(8,128)(2,1)} copy(bf16[256,4,8,256]{3,0,2,1:T(8,128)(2,1)} %bitcast.52) | data formatting | bytes 8388608 | tf_op jit(solution)/shard_map/jit(_take)/gather | solution.py:32
  144.0 0.0 copy-start.4
  144.0 0.0 copy-start.3
  144.0 0.0 copy-start.6
  144.0 6.2 %fusion = f32[4,256,256,1]{2,1,3,0:T(8,128)} fusion(bf16[4,8,256,256]{3,2,1,0:T(8,128)(2,1)} %param.13, bf16[256,4,8,256]{0,3,2,1:T(8,128)(2,1)} %copy.61, pred[4,8]{1,0:T(4,128)(4,1)S(1)} %copy.57, bf16[4,8]{1,0:T(4,128)(2,1)S(1)} %get-tuple-element.19), kind=kOutput, calls=%fused_computation.4 | convolution fusion | flops 1077936128 | bytes 9437280 | tf_op jit(solution)/shard_map/frkb,rkbo->fro/dot_general | solution.py:35
  150.2 0.0 reduce-scatter.4.cloned.1.call-update
  150.2 0.0 all-gather.5.cloned.1.call-start
  150.3 37.7 %reduce-scatter.4.cloned.1.call-done = f32[256,128]{0,1:T(8,128)} async-done(((f32[256,1024]{0,1:T(8,128)}), f32[256,128]{0,1:T(8,128)}) %reduce-scatter.4.cloned.1.call-update) | async-done | bytes 131088 | tf_op jit(solution)/shard_map/reduce_scatter | solution.py:38
  188.0 0.0 copy-done.4
  188.0 1.6 tanh_convert_fusion.1
  189.6 0.0 all-gather.5.cloned.1.call-update
  189.6 0.0 reduce-scatter.6.cloned.1.call-start
  189.7 0.0 copy-done.3
  189.7 0.1 reshape.206
  189.8 0.0 copy-done.6
  189.8 0.1 fusion.19
  189.9 56.9 %all-gather.5.cloned.1.call-done = bf16[256,4096]{0,1:T(8,128)(2,1)} async-done(((bf16[256,128]{0,1:T(8,128)(2,1)}), bf16[256,4096]{0,1:T(8,128)(2,1)}) %all-gather.5.cloned.1.call-update) | async-done | bytes 2097168 | tf_op jit(solution)/shard_map/all_gather | solution.py:40
  246.8 2.8 copy.64
  249.6 2.0 gather_fusion.1
  251.6 0.0 copy-start
  251.6 4.3 copy.65
  256.0 0.0 copy-done
  256.0 0.0 copy-start.2
  256.0 0.0 copy-start.5
  256.0 3.6 fusion.8
  259.6 0.0 reduce-scatter.6.cloned.1.call-update
  259.6 0.0 reduce-scatter.8.cloned.1.call-start
  259.7 0.1 reshape.208
  259.7 0.0 copy-done.2
  259.7 0.1 copy.68
  259.9 36.5 %reduce-scatter.6.cloned.1.call-done = f32[256,128]{0,1:T(8,128)} async-done(((f32[256,1024]{0,1:T(8,128)}), f32[256,128]{0,1:T(8,128)}) %reduce-scatter.6.cloned.1.call-update) | async-done | bytes 131088 | tf_op jit(solution)/shard_map/reduce_scatter | solution.py:48
  296.4 0.0 copy-done.5
  296.4 1.0 multiply_convert_fusion.3
  297.4 28.9 %all_gather.14 = bf16[256,1024]{0,1:T(8,128)(2,1)S(1)} all-gather(bf16[256,128]{0,1:T(8,128)(2,1)S(1)} %get-tuple-element.12), channel_id=1, replica_groups=mesh['out'=32,'in'=8] {'in'}, dimensions={1}, use_global_device_ids=true | all-gather | bytes 589824 | tf_op jit(solution)/shard_map/all_gather | solution.py:52
  326.2 2.8 fusion.6
  329.0 5.5 %copy.70 = f32[256,16,256]{2,1,0:T(8,128)} copy(f32[256,16,256]{0,2,1:T(8,128)} %bitcast.51) | data formatting | bytes 8388608 | tf_op jit(solution)/shard_map/reshape | solution.py:61
  334.5 4.3 convert_bitcast_fusion
  338.9 2.7 copy.86
  341.6 0.0 copy-start.1
  341.6 0.0 reduce-scatter.8.cloned.1.call-update
  341.6 0.7 copy.74
  342.4 3.7 multiply_convert_fusion.1
  346.0 88.3 %reduce-scatter.8.cloned.1.call-done = bf16[256,128]{0,1:T(8,128)(2,1)} async-done(((bf16[256,4096]{0,1:T(8,128)(2,1)}), bf16[256,128]{0,1:T(8,128)(2,1)}) %reduce-scatter.8.cloned.1.call-update) | async-done | bytes 65552 | tf_op jit(solution)/shard_map/reduce_scatter | solution.py:69
  434.3 0.0 copy-done.1
  434.3 0.9 multiply_convert_fusion.2
  435.2 29.0 %all_gather.15 = bf16[256,1024]{0,1:T(8,128)(2,1)S(1)} all-gather(bf16[256,128]{0,1:T(8,128)(2,1)S(1)} %multiply_convert_fusion.2), channel_id=1, replica_groups=mesh['out'=32,'in'=8] {'in'}, dimensions={1}, use_global_device_ids=true | all-gather | bytes 589824 | tf_op jit(solution)/shard_map/all_gather | solution.py:74
  464.2 5.5 %multiply_convert_fusion = bf16[4,8,256,256]{3,2,1,0:T(8,128)(2,1)} fusion(f32[4,8]{1,0:T(4,128)S(1)} %get-tuple-element.18, bf16[256,4,256,1]{0,2,3,1:T(8,128)(2,1)S(1)} %bitcast.60, bf16[256,4,8,256]{0,3,2,1:T(8,128)(2,1)} %copy.61, pred[4,8]{1,0:T(4,128)(4,1)S(1)} %copy.57), kind=kOutput, calls=%fused_computation.2 | convolution fusion | flops 1080033280 | bytes 8913056 | tf_op jit(solution)/shard_map/frkb,fro->rkbo/dot_general | solution.py:75
  (4 shorter events, 0.0 us)
Async XLA Ops:
  7.2 95.6 %all-gather.3.cloned.1.call-start = ((), (), s32[]{:S(2)}) async-start(), calls=%async_computation.3 | async-start | bytes 10813440 | tf_op jit(solution)/shard_map/all_gather | solution.py:28
  7.9 180.1 %reduce-scatter.4.cloned.1.call-start = ((), (), s32[]{:S(2)}) async-start(), calls=%async_computation.4 | async-start | bytes 1179648 | tf_op jit(solution)/shard_map/reduce_scatter | solution.py:38
  144.0 44.0 %copy-start.4 = (f32[128]{0:T(128)S(1)}, f32[128]{0:T(128)}, u32[]{:S(2)}) copy-start(f32[128]{0:T(128)} %param.14) | copy-start | bytes 1540
  144.0 45.7 %copy-start.3 = (s32[4,4]{1,0:T(4,128)S(1)}, s32[4,4]{1,0:T(4,128)}, u32[]{:S(2)}) copy-start(s32[4,4]{1,0:T(4,128)} %param.15) | copy-start | bytes 196
  144.0 45.8 %copy-start.6 = (s32[4,1]{0,1:T(1,128)S(1)}, s32[4,1]{0,1:T(1,128)}, u32[]{:S(2)}) copy-start(s32[4,1]{0,1:T(1,128)} %param.16) | copy-start | bytes 52
  150.2 96.5 %all-gather.5.cloned.1.call-start = ((), (), s32[]{:S(2)}) async-start(), calls=%async_computation.5 | async-start | bytes 2162688 | tf_op jit(solution)/shard_map/all_gather | solution.py:40
  189.6 106.7 %reduce-scatter.6.cloned.1.call-start = ((), (), s32[]{:S(2)}) async-start(), calls=%async_computation.6 | async-start | bytes 1179648 | tf_op jit(solution)/shard_map/reduce_scatter | solution.py:48
  251.6 4.3 copy-start
  256.0 3.8 copy-start.2
  256.0 40.4 %copy-start.5 = (f32[128]{0:T(128)S(1)}, f32[128]{0:T(128)}, u32[]{:S(2)}) copy-start(f32[128]{0:T(128)} %param.18) | copy-start | bytes 1540
  259.6 174.7 %reduce-scatter.8.cloned.1.call-start = ((), (), s32[]{:S(2)}) async-start(), calls=%async_computation.7 | async-start | bytes 2162688 | tf_op jit(solution)/shard_map/reduce_scatter | solution.py:69
  341.6 92.7 %copy-start.1 = (f32[256,128]{0,1:T(8,128)S(1)}, f32[256,128]{0,1:T(8,128)}, u32[]{:S(2)}) copy-start(f32[256,128]{0,1:T(8,128)} %reduce-scatter.4.cloned.1.call-done) | copy-start | bytes 393220
Sparse Core Ops, SparseCore 0:
  10.5 92.1 all-gather.2
  150.4 37.5 reduce-scatter.3
  191.1 55.6 all-gather.4
  259.7 36.5 reduce-scatter.5
  341.7 92.4 reduce-scatter.7
where the time goes:
time: 478 us; the launch traced here: 476 us
  waiting for transfers between devices  313 us (65%)
  local copies, waits for them, and re-layouts  59.9 us (13%)
  blocking collectives  57.9 us (12%)
  matrix products  26.1 us (5%)
  between operations  13.9 us (3%)
  other arithmetic  5.16 us (1%)
    all_gather x1, waiting for transfers between devices, shards(): gathered = lax.all_gather(slopes, 'out', axis=0, tiled=True)  93.1 us
    reduce_scatter x1, waiting for transfers between devices, shards(): lax.psum_scatter(spread.astype(jnp.bfloat16), 'out', scatter_dimension=1,...  88.3 us
    all_gather x1, waiting for transfers between devices, shards(): second_input = lax.all_gather(hidden_first, 'out', axis=1, tiled=True)  56.9 us
    reduce_scatter x1, waiting for transfers between devices, shards(): lax.psum_scatter(partial_first, 'in', scatter_dimension=1, tiled=True)  37.7 us
    reduce_scatter x1, waiting for transfers between devices, shards(): lax.psum_scatter(partial_second, 'in', scatter_dimension=1, tiled=True)  36.5 us
    all_gather x1, blocking collectives, shards(): lax.all_gather(delta_first, 'in', axis=1, tiled=True)  29 us
    all_gather x1, blocking collectives, shards(): lax.all_gather(delta_second, 'in', axis=1, tiled=True)  28.9 us
    reshape x1, local copies, waits for them, and re-layouts, shards(): slope_blocks = gathered.reshape(frames, -1, BLK)  14.4 us
  transfers between devices with their start and end apart: 5, of which 5 were waited for; matrix products, arithmetic and copies ran while one was open for 1% of the time, Pallas kernels for 0%

commit v1 on v0

--- a/solution.py
+++ b/solution.py
@@ -25,7 +25,9 @@
     live_second = jnp.arange(KD2, dtype=jnp.int32)[None, :] < count_second
     masked_first = weight_first * live_first.astype(jnp.bfloat16)[:, :, None, None]
     masked_second = weight_second * live_second.astype(jnp.bfloat16)[:, :, None, None]
-    gathered = lax.all_gather(slopes, "out", axis=0, tiled=True)
+    gathered = jnp.concatenate(
+        lax.all_to_all(jnp.stack([slopes] * lax.axis_size("out")), "out", 0, 0), axis=0
+    )
     frames = gathered.shape[0]
     slope_blocks = gathered.reshape(frames, -1, BLK)
     own_cols = lax.dynamic_slice_in_dim(cols_first, lax.axis_index("out") * rows, rows, 0)

time: 478 us -> 624 us (1.31)
  waiting for transfers between devices: 313 us -> 448 us
  starting transfers between devices: 0.2 us -> 11.9 us
    all_to_all x0 -> x1, waiting for transfers between devices: none -> 232 us  [shards(): lax.all_to_all(jnp.stack([slopes] * lax.axis_size('out')), 'out', 0, 0)]
    all_gather x1 -> x0, waiting for transfers between devices: 93.1 us -> none  [shards(): gathered = lax.all_gather(slopes, 'out', axis=0, tiled=True)]
    another operation x0 -> x2, local copies, waits for them, and re-layouts: none -> 17.8 us  [the longest x1 11.8 us: shards(): slope_blocks = gathered.reshape(frames, -1, BLK)]
    reshape x1 -> x0, local copies, waits for them, and re-layouts: 14.4 us -> none  [shards(): slope_blocks = gathered.reshape(frames, -1, BLK)]
    all_gather x1 -> x0, local copies, waits for them, and re-layouts: 13.8 us -> none  [shards(): gathered = lax.all_gather(slopes, 'out', axis=0, tiled=True)]
    all_to_all x0 -> x1, starting transfers between devices: none -> 11.6 us  [shards(): lax.all_to_all(jnp.stack([slopes] * lax.axis_size('out')), 'out', 0, 0)]
    unnamed x16 -> x21, local copies, waits for them, and re-layouts: 0.87 us -> 12 us
where the time goes in v1:
time: 624 us; the launch traced here: 623 us
  waiting for transfers between devices  448 us (72%)
  local copies, waits for them, and re-layouts  60.7 us (10%)
  blocking collectives  57.9 us (9%)
  matrix products  26.1 us (4%)
  between operations  13.9 us (2%)
  starting transfers between devices  11.9 us (2%)
    all_to_all x1, waiting for transfers between devices, shards(): lax.all_to_all(jnp.stack([slopes] * lax.axis_size('out')), 'out', 0, 0)  232 us
    reduce_scatter x1, waiting for transfers between devices, shards(): lax.psum_scatter(spread.astype(jnp.bfloat16), 'out', scatter_dimension=1,...  88.4 us
    all_gather x1, waiting for transfers between devices, shards(): second_input = lax.all_gather(hidden_first, 'out', axis=1, tiled=True)  56.7 us
    reduce_scatter x1, waiting for transfers between devices, shards(): lax.psum_scatter(partial_second, 'in', scatter_dimension=1, tiled=True)  36.5 us
    reduce_scatter x1, waiting for transfers between devices, shards(): lax.psum_scatter(partial_first, 'in', scatter_dimension=1, tiled=True)  34.5 us
    all_gather x1, blocking collectives, shards(): lax.all_gather(delta_first, 'in', axis=1, tiled=True)  29 us
    all_gather x1, blocking collectives, shards(): lax.all_gather(delta_second, 'in', axis=1, tiled=True)  28.9 us
    gather x2, local copies, waits for them, and re-layouts, shards(): jnp.take(slope_blocks, own_cols.reshape(-1), axis=1)  13 us
  transfers between devices with their start and end apart: 5, of which 5 were waited for; matrix products, arithmetic and copies ran while one was open for 1% of the time, Pallas kernels for 0%

profile of v1, /device:TPU:24, one launch (start us, length us, event | category | flops | bytes accessed | tf_op | source)
XLA Modules:
  0.0 622.7 jit_solution(613765203094674321)
XLA Ops:
  7.2 6.0 stack.2
  13.1 0.0 copy-start.4
  13.1 0.0 copy-start.7
  13.2 11.6 %all-to-all-start = ((bf16[32,8,20480]{2,1,0:T(8,128)(2,1)}), bf16[32,8,20480]{2,1,0:T(8,128)(2,1)}, u32[]{:S(2)}, u32[]{:S(2)}) async-start(bf16[32,8,20480]{2,1,0:T(8,128)(2,1)} %stack.2), calls=%async_computation | async-start | bytes 20971520 | tf_op jit(solution)/shard_map/all_to_all | solution.py:29
  24.7 0.0 reduce-scatter.4.cloned.1.call-start
  24.8 0.0 copy-done.4
  24.8 0.1 compare_and_fusion
  24.9 0.1 copy.39
  24.9 0.1 reshape.201
  25.0 0.1 copy.38
  25.1 0.0 copy-done.7
  25.2 0.1 fusion.17
  25.2 232.3 %all-to-all-done = bf16[32,8,20480]{2,1,0:T(8,128)(2,1)} async-done(((bf16[32,8,20480]{2,1,0:T(8,128)(2,1)}), bf16[32,8,20480]{2,1,0:T(8,128)(2,1)}, u32[]{:S(2)}, u32[]{:S(2)}) %all-to-all-start) | async-done | bytes 10485792 | tf_op jit(solution)/shard_map/all_to_all | solution.py:29
  257.6 11.2 %copy.71 = bf16[32,8,80,256]{3,2,1,0:T(8,128)(2,1)} copy(bf16[32,8,80,256]{3,1,2,0:T(8,128)(2,1)} %bitcast.41) | data formatting | bytes 20971520
  268.7 11.8 %copy.40 = bf16[256,80,256]{2,0,1:T(8,128)(2,1)} copy(bf16[256,80,256]{2,1,0:T(8,128)(2,1)} %bitcast.52) | data formatting | bytes 20971520 | tf_op jit(solution)/shard_map/reshape;reshape | solution.py:32
  280.5 6.8 %gather_fusion = bf16[32,256,256]{2,1,0:T(8,128)(2,1)} fusion(bf16[256,80,256]{2,0,1:T(8,128)(2,1)} %copy.40, s32[1024]{0:T(1024)S(1)} %pad_clamp_fusion.1), kind=kCustom, calls=%fused_computation | custom fusion | bytes 8388736 | tf_op jit(solution)/shard_map/jit(_take)/gather | solution.py:34
  287.3 6.2 copy.41
  293.5 0.0 copy-start.5
  293.5 0.0 copy-start.3
  293.5 0.0 copy-start.8
  293.5 6.2 %fusion = f32[4,256,256,1]{2,1,3,0:T(8,128)} fusion(bf16[4,8,256,256]{3,2,1,0:T(8,128)(2,1)} %param.13, bf16[256,4,8,256]{0,3,2,1:T(8,128)(2,1)} %copy.41, pred[4,8]{1,0:T(4,128)(4,1)S(1)} %copy.38, bf16[4,8]{1,0:T(4,128)(2,1)S(1)} %get-tuple-element.16), kind=kOutput, calls=%fused_computation.4 | convolution fusion | flops 1077936128 | bytes 9437280 | tf_op jit(solution)/shard_map/frkb,rkbo->fro/dot_general | solution.py:37
  299.8 0.0 reduce-scatter.4.cloned.1.call-update
  299.8 0.0 all-gather.2.cloned.1.call-start
  299.8 34.5 %reduce-scatter.4.cloned.1.call-done = f32[256,128]{0,1:T(8,128)} async-done(((f32[256,1024]{0,1:T(8,128)}), f32[256,128]{0,1:T(8,128)}) %reduce-scatter.4.cloned.1.call-update) | async-done | bytes 131088 | tf_op jit(solution)/shard_map/reduce_scatter | solution.py:40
  334.3 0.0 copy-done.5
  334.3 1.6 tanh_convert_fusion.1
  336.0 0.0 all-gather.2.cloned.1.call-update
  336.0 0.2 reduce-scatter.6.cloned.1.call-start
  336.2 0.0 copy-done.3
  336.2 0.1 reshape.204
  336.3 0.0 copy-done.8
  336.3 0.1 fusion.19
  336.4 56.7 %all-gather.2.cloned.1.call-done = bf16[256,4096]{0,1:T(8,128)(2,1)} async-done(((bf16[256,128]{0,1:T(8,128)(2,1)}), bf16[256,4096]{0,1:T(8,128)(2,1)}) %all-gather.2.cloned.1.call-update) | async-done | bytes 2097168 | tf_op jit(solution)/shard_map/all_gather | solution.py:42
  393.1 2.8 copy.44
  395.9 2.0 gather_fusion.1
  397.9 0.0 copy-start
  397.9 4.3 copy.45
  402.3 0.0 copy-done
  402.3 0.0 copy-start.2
  402.3 0.0 copy-start.6
  402.3 3.6 fusion.8
  405.9 0.0 reduce-scatter.6.cloned.1.call-update
  405.9 0.0 reduce-scatter.8.cloned.1.call-start
  405.9 0.1 reshape.206
  406.0 0.0 copy-done.2
  406.0 0.1 copy.48
  406.1 36.5 %reduce-scatter.6.cloned.1.call-done = f32[256,128]{0,1:T(8,128)} async-done(((f32[256,1024]{0,1:T(8,128)}), f32[256,128]{0,1:T(8,128)}) %reduce-scatter.6.cloned.1.call-update) | async-done | bytes 131088 | tf_op jit(solution)/shard_map/reduce_scatter | solution.py:50
  442.6 0.0 copy-done.6
  442.6 1.0 multiply_convert_fusion.3
  443.7 28.9 %all_gather.10 = bf16[256,1024]{0,1:T(8,128)(2,1)S(1)} all-gather(bf16[256,128]{0,1:T(8,128)(2,1)S(1)} %get-tuple-element.9), channel_id=1, replica_groups=mesh['out'=32,'in'=8] {'in'}, dimensions={1}, use_global_device_ids=true | all-gather | bytes 589824 | tf_op jit(solution)/shard_map/all_gather | solution.py:54
  472.5 2.8 fusion.6
  475.3 5.5 copy.50
  480.8 4.3 convert_bitcast_fusion
  485.1 2.7 copy.66
  487.9 0.0 copy-start.1
  487.9 0.0 reduce-scatter.8.cloned.1.call-update
  487.9 0.7 copy.54
  488.6 3.7 multiply_convert_fusion.1
  492.3 88.4 %reduce-scatter.8.cloned.1.call-done = bf16[256,128]{0,1:T(8,128)(2,1)} async-done(((bf16[256,4096]{0,1:T(8,128)(2,1)}), bf16[256,128]{0,1:T(8,128)(2,1)}) %reduce-scatter.8.cloned.1.call-update) | async-done | bytes 65552 | tf_op jit(solution)/shard_map/reduce_scatter | solution.py:71
  580.7 0.0 copy-done.1
  580.7 0.9 multiply_convert_fusion.2
  581.6 29.0 %all_gather.11 = bf16[256,1024]{0,1:T(8,128)(2,1)S(1)} all-gather(bf16[256,128]{0,1:T(8,128)(2,1)S(1)} %multiply_convert_fusion.2), channel_id=1, replica_groups=mesh['out'=32,'in'=8] {'in'}, dimensions={1}, use_global_device_ids=true | all-gather | bytes 589824 | tf_op jit(solution)/shard_map/all_gather | solution.py:76
  610.6 5.5 multiply_convert_fusion
  (4 shorter events, 0.0 us)
Async XLA Ops:
  13.1 11.6 %copy-start.4 = (s32[128,8]{0,1:T(8,128)S(1)}, s32[128,8]{0,1:T(8,128)}, u32[]{:S(2)}) copy-start(s32[128,8]{0,1:T(8,128)} %param.11) | copy-start | bytes 12292
  13.1 12.0 %copy-start.7 = (s32[4,1]{0,1:T(1,128)S(1)}, s32[4,1]{0,1:T(1,128)}, u32[]{:S(2)}) copy-start(s32[4,1]{0,1:T(1,128)} %param.12) | copy-start | bytes 52
  13.2 244.4 %all-to-all-start = ((bf16[32,8,20480]{2,1,0:T(8,128)(2,1)}), bf16[32,8,20480]{2,1,0:T(8,128)(2,1)}, u32[]{:S(2)}, u32[]{:S(2)}) async-start(bf16[32,8,20480]{2,1,0:T(8,128)(2,1)} %stack.2), calls=%async_computation | async-start | bytes 20971520 | tf_op jit(solution)/shard_map/all_to_all | solution.py:29
  24.7 309.6 %reduce-scatter.4.cloned.1.call-start = ((), (), s32[]{:S(2)}) async-start(), calls=%async_computation.4 | async-start | bytes 1179648 | tf_op jit(solution)/shard_map/reduce_scatter | solution.py:40
  293.5 40.8 %copy-start.5 = (f32[128]{0:T(128)S(1)}, f32[128]{0:T(128)}, u32[]{:S(2)}) copy-start(f32[128]{0:T(128)} %param.14) | copy-start | bytes 1540
  293.5 42.7 %copy-start.3 = (s32[4,4]{1,0:T(4,128)S(1)}, s32[4,4]{1,0:T(4,128)}, u32[]{:S(2)}) copy-start(s32[4,4]{1,0:T(4,128)} %param.15) | copy-start | bytes 196
  293.5 42.8 %copy-start.8 = (s32[4,1]{0,1:T(1,128)S(1)}, s32[4,1]{0,1:T(1,128)}, u32[]{:S(2)}) copy-start(s32[4,1]{0,1:T(1,128)} %param.16) | copy-start | bytes 52
  299.8 93.3 %all-gather.2.cloned.1.call-start = ((), (), s32[]{:S(2)}) async-start(), calls=%async_computation.5 | async-start | bytes 2162688 | tf_op jit(solution)/shard_map/all_gather | solution.py:42
  336.0 106.7 %reduce-scatter.6.cloned.1.call-start = ((), (), s32[]{:S(2)}) async-start(), calls=%async_computation.6 | async-start | bytes 1179648 | tf_op jit(solution)/shard_map/reduce_scatter | solution.py:50
  397.9 4.3 copy-start
  402.3 3.8 copy-start.2
  402.3 40.4 %copy-start.6 = (f32[128]{0:T(128)S(1)}, f32[128]{0:T(128)}, u32[]{:S(2)}) copy-start(f32[128]{0:T(128)} %param.18) | copy-start | bytes 1540
  405.9 174.8 %reduce-scatter.8.cloned.1.call-start = ((), (), s32[]{:S(2)}) async-start(), calls=%async_computation.7 | async-start | bytes 2162688 | tf_op jit(solution)/shard_map/reduce_scatter | solution.py:71
  487.9 92.8 %copy-start.1 = (f32[256,128]{0,1:T(8,128)S(1)}, f32[256,128]{0,1:T(8,128)}, u32[]{:S(2)}) copy-start(f32[256,128]{0,1:T(8,128)} %reduce-scatter.4.cloned.1.call-done) | copy-start | bytes 393220
Sparse Core Ops, SparseCore 0:
  299.9 34.3 reduce-scatter.3
  337.5 55.5 all-gather.1
  406.0 36.5 reduce-scatter.5
  488.0 92.6 reduce-scatter.7
